TPU v7x, 512 devices: a whole 4x8x8 slice. The times are simulated.
512 devices in a mesh: tp: 64 (over y, z_hi, core), ep: 8 (over x, z_lo).
Axes of the slice: x: 4, y: 8, z: 8 (z_hi: 4, z_lo: 2; z = z_hi * 2 + z_lo), core: 2. Of those that a mesh axis runs over, the one named last changes fastest.
Arguments:
- residual: bfloat16 [8, 7168, 256], P('ep', 'tp')
- out_grad: bfloat16 [8, 7168, 256], P('ep', 'tp'), may hold values from -6 to 6
- norm_gain: float32 [7168], P('tp'), may hold values from 0.25 to 1.75
- context: bfloat16 [8, 16384, 256], P('ep', 'tp'), may hold values from -0.3125 to 0.3125
- w_out: bfloat16 [7168, 16384], P('ep', 'tp'), may hold values from -0.046875 to 0.046875
- w_gate: bfloat16 [8, 7168, 2048], P('ep', 'tp'), may hold values from -0.0625 to 0.0625
- w_up: bfloat16 [8, 7168, 2048], P('ep', 'tp'), may hold values from -0.0625 to 0.0625
- w_down: bfloat16 [8, 7168, 2048], P('ep', 'tp'), may hold values from -0.125 to 0.125
- slot_token: int32 [8, 8, 8], P('ep'), may hold values from 0 to 255, as said below
- slot_count: int32 [8, 8], P('ep'), may hold values from 1 to 8, as said below
- slot_gate: float32 [8, 8, 8], P('ep'), may hold values from 0.25 to 2.5
Outputs:
- resid_grad: bfloat16 [8, 7168, 256], P('ep', 'tp')
- context_grad: bfloat16 [8, 16384, 256], P('ep', 'tp')
- w_out_grad: bfloat16 [7168, 16384], P('ep', 'tp')
- gate_grad: bfloat16 [8, 7168, 2048], P('ep', 'tp')
- up_grad: bfloat16 [8, 7168, 2048], P('ep', 'tp')
- down_grad: bfloat16 [8, 7168, 2048], P('ep', 'tp')
Inputs may be any that keep to these rules, and one draw needn't show every extreme that they name: `slot_token`: within one group and expert the 8 token positions are distinct; slots at or beyond slot_count are unused. `slot_count`: in every draw one expert has 8 tokens from every group.
All inputs are finite; a program needn't handle non-finite values.
Results may differ from a plain program's by a relative error of at most 0.014.
Values may be sent and summed in bfloat16 or wider, within the bound.
A program may use at most 64 MiB of HBM per device.

v0:
```python
import jax
import jax.numpy as jnp
from jax import lax
from jax.sharding import PartitionSpec as P

norm_eps = 1e-06


def contract_rows(left, right):
    return lax.dot_general(
        left, right, (((0,), (0,)), ((), ())), preferred_element_type=jnp.float32
    )


def contract_cols(left, right):
    return lax.dot_general(
        left, right, (((1,), (1,)), ((), ())), preferred_element_type=jnp.float32
    )


def activate(pre_gate, pre_up, hid_grad):
    sigmoid_gate = jax.nn.sigmoid(pre_gate)
    silu_gate = pre_gate * sigmoid_gate
    hidden = (silu_gate * pre_up).astype(jnp.bfloat16)
    d_gate = (hid_grad * pre_up * sigmoid_gate * (1.0 + pre_gate * (1.0 - sigmoid_gate))).astype(
        jnp.bfloat16
    )
    d_up = (hid_grad * silu_gate).astype(jnp.bfloat16)
    return (hidden, d_gate, d_up)


def shards(
    residual,
    out_grad,
    norm_gain,
    context,
    w_out,
    w_gate,
    w_up,
    w_down,
    slot_token,
    slot_count,
    slot_gate,
):
    tp_count = lax.axis_size("tp")
    stream = residual[0].astype(jnp.float32)
    grad_in = out_grad[0].astype(jnp.float32)
    feat_share, group_rows = stream.shape
    features = feat_share * tp_count
    square = lax.psum(jnp.sum(stream * stream, axis=0), "tp")
    inv_rms = lax.rsqrt(square / features + norm_eps)[None, :]
    normed = stream * inv_rms
    gain_col = norm_gain[:, None]
    inputs = (normed * gain_col).astype(jnp.bfloat16)
    slot_table = slot_token[0]
    capacity = slot_table.shape[1]
    live_mask = jnp.arange(capacity)[None, :] < slot_count[0][:, None]
    one_hot = (
        (slot_table[:, :, None] == jnp.arange(group_rows)[None, None, :]) & live_mask[:, :, None]
    ).astype(jnp.bfloat16)
    send_x = jnp.einsum("dt,ect->edc", inputs, one_hot, preferred_element_type=jnp.float32).astype(
        jnp.bfloat16
    )
    go_rows = jnp.einsum("dt,ect->edc", out_grad[0], one_hot, preferred_element_type=jnp.float32)
    send_go = (slot_gate[0][:, None, :] * go_rows).astype(jnp.bfloat16)
    recv_x, recv_go = (
        lax.all_to_all(send_x, "ep", split_axis=0, concat_axis=2, tiled=True),
        lax.all_to_all(send_go, "ep", split_axis=0, concat_axis=2, tiled=True),
    )
    rows_x = recv_x[0]
    rows_go = recv_go[0]
    gate_w = w_gate[0]
    up_w = w_up[0]
    down_w = w_down[0]
    gate_part = contract_rows(rows_x, gate_w)
    up_part = contract_rows(rows_x, up_w)
    hid_part = contract_rows(rows_go, down_w)
    pre_gate, pre_up, hid_grad = lax.psum((gate_part, up_part, hid_part), "tp")
    hidden, d_gate, d_up = activate(pre_gate, pre_up, hid_grad)
    down_grad = jnp.dot(rows_go, hidden, preferred_element_type=jnp.float32).astype(jnp.bfloat16)[
        None
    ]
    gate_grad = jnp.dot(rows_x, d_gate, preferred_element_type=jnp.float32).astype(jnp.bfloat16)[
        None
    ]
    up_grad = jnp.dot(rows_x, d_up, preferred_element_type=jnp.float32).astype(jnp.bfloat16)[None]
    slot_back = (contract_cols(gate_w, d_gate) + contract_cols(up_w, d_up)).astype(jnp.bfloat16)
    returned = lax.all_to_all(slot_back[None], "ep", split_axis=2, concat_axis=0, tiled=True)
    in_grad = jnp.einsum(
        "edc,ect->dt", returned, one_hot, preferred_element_type=jnp.float32
    ).astype(jnp.bfloat16)
    scaled = in_grad.astype(jnp.float32) * gain_col
    dots = lax.psum(jnp.sum(scaled * normed, axis=0), "tp")
    resid = (grad_in + inv_rms * (scaled - normed * (dots / features)[None, :])).astype(
        jnp.bfloat16
    )
    full_grad = lax.all_gather(resid, "tp", axis=0, tiled=True)
    grad_block = lax.all_to_all(full_grad, "ep", split_axis=0, concat_axis=1, tiled=True)
    ctx_local = context[0]
    ctx_all = lax.all_gather(ctx_local, "ep", axis=1, tiled=True)
    weight_sum = contract_cols(grad_block, ctx_all)
    ctx_total = contract_rows(lax.all_gather(w_out, "ep", axis=0, tiled=True), full_grad)
    return (
        resid[None],
        ctx_total.astype(jnp.bfloat16)[None],
        weight_sum.astype(jnp.bfloat16),
        gate_grad,
        up_grad,
        down_grad,
    )


def solution(mesh):
    return jax.shard_map(
        shards,
        mesh=mesh,
        in_specs=(
            P("ep", "tp", None),
            P("ep", "tp", None),
            P("tp"),
            P("ep", "tp", None),
            P("ep", "tp"),
            P("ep", "tp", None),
            P("ep", "tp", None),
            P("ep", "tp", None),
            P("ep", None, None),
            P("ep", None),
            P("ep", None, None),
        ),
        out_specs=(
            P("ep", "tp", None),
            P("ep", "tp", None),
            P("ep", "tp"),
            P("ep", "tp", None),
            P("ep", "tp", None),
            P("ep", "tp", None),
        ),
        check_vma=False,
    )
```

profile of v0, /device:TPU:2, one launch (start us, length us, event | category | flops | bytes accessed | tf_op | source)
XLA Modules:
  0.0 1152.4 jit_solution(9309882180991946875)
XLA Ops:
  7.2 0.9 fusion.32
  8.1 150.2 %psum.35 = f32[256]{0:T(256)S(1)} all-reduce(f32[256]{0:T(256)S(1)} %fusion.32), channel_id=1, replica_groups=mesh['tp'=64,'ep'=8] {'tp'}, use_global_device_ids=true, to_apply=%region_1.0 | all-reduce | flops 256 | bytes 2048 | tf_op jit(solution)/shard_map/psum | solution.py:50
  158.3 0.7 iota_compare_fusion.1
  159.1 1.6 fusion.9
  160.7 5.7 all-to-all-start.1
  166.5 1.6 fusion.11
  168.1 3.1 all-to-all-done.1
  171.2 4.7 all-to-all-start
  175.9 1.0 fusion.16
  177.0 2.1 fusion.19
  179.1 1.7 all-to-all-done
  180.7 2.0 fusion.21
  182.8 554.5 %all-reduce.3.cloned.1.call-done = (f32[64,2048]{1,0:T(8,128)}, f32[64,2048]{1,0:T(8,128)}, f32[64,2048]{1,0:T(8,128)}) async-done(((f32[64,2048]{1,0:T(8,128)}, f32[64,2048]{1,0:T(8,128)}, f32[64,2048]{1,0:T(8,128)}), (f32[64,2048]{1,0:T(8,128)}, f32[64,2048]{1,0:T(8,128)}, f32[64,2048]{1,0:T(8,128)})) %all-reduce.3.cloned.1.call-update) | async-done | bytes 1572880 | tf_op jit(solution)/shard_map/psum | solution.py:78
  737.3 1.6 multiply_convert_fusion.1
  739.6 0.5 broadcast.36
  740.1 0.7 reduce
  740.9 9.5 all_to_all.67
  750.9 142.3 %psum.39 = f32[256]{0:T(256)S(1)} all-reduce(f32[256]{0:T(256)S(1)} %get-tuple-element.35), channel_id=1, replica_groups=mesh['tp'=64,'ep'=8] {'tp'}, use_global_device_ids=true, to_apply=%region_6.0 | all-reduce | flops 256 | bytes 2048 | tf_op jit(solution)/shard_map/psum | solution.py:93
  893.2 0.7 fusion.31
  893.9 0.7 all-gather.7.cloned.1.call-update
  894.6 78.9 %all-gather.5.cloned.1.call-done = bf16[7168,256]{1,0:T(8,128)(2,1)} async-done(((bf16[112,256]{1,0:T(8,128)(2,1)}), bf16[7168,256]{1,0:T(8,128)(2,1)}) %all-gather.5.cloned.1.call-update) | async-done | bytes 3670032 | tf_op jit(solution)/shard_map/all_gather | solution.py:97
  973.5 6.2 copy.32
  979.8 6.5 all-to-all-start.3
  986.3 0.6 all-gather.9.cloned.1.call-update
  986.9 1.1 fusion
  987.9 1.1 fusion.1
  989.0 1.1 fusion.2
  990.1 107.2 %all-gather.7.cloned.1.call-done = bf16[7168,256]{1,0:T(8,128)(2,1)} async-done(((bf16[896,256]{1,0:T(8,128)(2,1)}), bf16[7168,256]{1,0:T(8,128)(2,1)}) %all-gather.7.cloned.1.call-update) | async-done | bytes 3670032 | tf_op jit(solution)/shard_map/all_gather | solution.py:102
  1097.3 4.3 fusion.3
  1101.6 0.8 copy.33
  1102.4 39.3 %all-gather.9.cloned.1.call-done = bf16[1,256,2048]{2,1,0:T(8,128)(2,1)} async-done(((bf16[1,256,256]{2,1,0:T(8,128)(2,1)}), bf16[1,256,2048]{2,1,0:T(8,128)(2,1)}) %all-gather.9.cloned.1.call-update) | async-done | bytes 1048592 | tf_op jit(solution)/shard_map/all_gather | solution.py:100
  1141.6 4.3 convolution_convert_fusion.3
  (31 shorter events, 1.2 us)
Async XLA Ops:
  7.2 168.8 %copy-start = (bf16[1,112,2048]{2,1,0:T(8,128)(2,1)S(1)}, bf16[1,112,2048]{2,1,0:T(8,128)(2,1)}, u32[]{:S(2)}) copy-start(bf16[1,112,2048]{2,1,0:T(8,128)(2,1)} %param.16) | copy-start | bytes 1376260
  160.7 10.5 all-to-all-start.1
  171.2 9.5 all-to-all-start
  175.9 563.3 %copy-start.1 = (bf16[1,112,2048]{2,1,0:T(8,128)(2,1)S(1)}, bf16[1,112,2048]{2,1,0:T(8,128)(2,1)}, u32[]{:S(2)}) copy-start(bf16[1,112,2048]{2,1,0:T(8,128)(2,1)} %param.17) | copy-start | bytes 1376260
  175.9 561.4 %all-reduce.3.cloned.1.call-start = ((), (), s32[]{:S(2)}) async-start(), calls=%async_computation.7 | async-start | bytes 3145728 | tf_op jit(solution)/shard_map/psum | solution.py:78
  176.9 573.6 %copy-start.4 = (bf16[1,112,256]{2,1,0:T(8,128)(2,1)S(1)}, bf16[1,112,256]{2,1,0:T(8,128)(2,1)}, u32[]{:S(2)}) copy-start(bf16[1,112,256]{2,1,0:T(8,128)(2,1)} %param.11) | copy-start | bytes 172036
  176.9 573.6 %copy-start.6 = (s32[1,8,8]{2,1,0:T(8,128)S(1)}, s32[1,8,8]{2,1,0:T(8,128)}, u32[]{:S(2)}) copy-start(s32[1,8,8]{2,1,0:T(8,128)} %param.19) | copy-start | bytes 772
  177.0 573.6 %copy-start.7 = (f32[112]{0:T(128)S(1)}, f32[112]{0:T(128)}, u32[]{:S(2)}) copy-start(f32[112]{0:T(128)} %param.13) | copy-start | bytes 1348
  177.0 716.3 %copy-start.5 = (bf16[1,112,256]{2,1,0:T(8,128)(2,1)S(1)}, bf16[1,112,256]{2,1,0:T(8,128)(2,1)}, u32[]{:S(2)}) copy-start(bf16[1,112,256]{2,1,0:T(8,128)(2,1)} %param.12) | copy-start | bytes 172036
  182.8 790.7 %all-gather.5.cloned.1.call-start = ((), (), s32[]{:S(2)}) async-start(), calls=%async_computation.4 | async-start | bytes 3727360 | tf_op jit(solution)/shard_map/all_gather | solution.py:97
  893.9 203.4 %all-gather.7.cloned.1.call-start = ((), (), s32[]{:S(2)}) async-start(), calls=%async_computation.5 | async-start | bytes 4128768 | tf_op jit(solution)/shard_map/all_gather | solution.py:102
  979.8 9.3 copy-start.2
  979.8 9.3 copy-start.3
  979.8 161.9 %all-to-all-start.3 = ((bf16[8,896,256]{1,2,0:T(8,128)(2,1)}), bf16[8,896,256]{1,2,0:T(8,128)(2,1)}, u32[]{:S(2)}, u32[]{:S(2)}) async-start(bf16[8,896,256]{1,2,0:T(8,128)(2,1)} %copy.32), calls=%async_computation.3 | async-start | bytes 7340032 | tf_op jit(solution)/shard_map/all_to_all | solution.py:98
  986.3 155.3 %all-gather.9.cloned.1.call-start = ((), (), s32[]{:S(2)}) async-start(), calls=%async_computation.6 | async-start | bytes 1179648 | tf_op jit(solution)/shard_map/all_gather | solution.py:100
Sparse Core Ops, SparseCore 0:
  182.9 554.3 all-reduce.2
  894.0 79.4 all-gather.4
  975.8 121.4 all-gather.6
  1099.3 42.2 all-gather.8
where the time goes:
time: 1150 us
  waiting for transfers between devices  786 us (68%)
  blocking collectives  302 us (26%)
  matrix products  21.1 us (2%)
  starting transfers between devices  17.1 us (1%)
  between operations  13.9 us (1%)
    psum x1, waiting for transfers between devices, shards(): pre_gate, pre_up, hid_grad = lax.psum((gate_part, up_part, hid_part), 'tp')  555 us
    psum x1, blocking collectives, shards(): square = lax.psum(jnp.sum(stream * stream, axis=0), 'tp')  150 us
    psum x1, blocking collectives, shards(): dots = lax.psum(jnp.sum(scaled * normed, axis=0), 'tp')  142 us
    all_gather x1, waiting for transfers between devices, shards(): lax.all_gather(w_out, 'ep', axis=0, tiled=True)  107 us
    all_gather x1, waiting for transfers between devices, shards(): full_grad = lax.all_gather(resid, 'tp', axis=0, tiled=True)  78.9 us
    all_gather x1, waiting for transfers between devices, shards(): ctx_all = lax.all_gather(ctx_local, 'ep', axis=1, tiled=True)  39.3 us
  transfers between devices with their start and end apart: 7, of which 6 were waited for; matrix products, arithmetic and copies ran while one was open for 2% of the time, Pallas kernels for 0%

commit v1 on v0

--- a/solution.py
+++ b/solution.py
@@ -90,7 +90,8 @@
         "edc,ect->dt", returned, one_hot, preferred_element_type=jnp.float32
     ).astype(jnp.bfloat16)
     scaled = in_grad.astype(jnp.float32) * gain_col
-    dots = lax.psum(jnp.sum(scaled * normed, axis=0), "tp")
+    x_local = jnp.sum(scaled * normed, axis=0)
+    dots = jnp.sum(lax.all_gather(x_local, "tp"), 0)
     resid = (grad_in + inv_rms * (scaled - normed * (dots / features)[None, :])).astype(
         jnp.bfloat16
     )

time: 1150 us -> 1090 us (0.948)
  blocking collectives: 302 us -> 240 us
    psum x1 -> x0, blocking collectives: 142 us -> none  [shards(): dots = lax.psum(jnp.sum(scaled * normed, axis=0), 'tp')]
    all_gather x0 -> x1, blocking collectives: none -> 80.4 us  [shards(): dots = jnp.sum(lax.all_gather(x_local, 'tp'), 0)]
where the time goes in v1:
time: 1090 us
  waiting for transfers between devices  786 us (72%)
  blocking collectives  240 us (22%)
  matrix products  21.1 us (2%)
  starting transfers between devices  17.1 us (2%)
  between operations  13.9 us (1%)
    psum x1, waiting for transfers between devices, shards(): pre_gate, pre_up, hid_grad = lax.psum((gate_part, up_part, hid_part), 'tp')  555 us
    psum x1, blocking collectives, shards(): square = lax.psum(jnp.sum(stream * stream, axis=0), 'tp')  150 us
    all_gather x1, waiting for transfers between devices, shards(): lax.all_gather(w_out, 'ep', axis=0, tiled=True)  107 us
    all_gather x1, blocking collectives, shards(): dots = jnp.sum(lax.all_gather(x_local, 'tp'), 0)  80.4 us
    all_gather x1, waiting for transfers between devices, shards(): full_grad = lax.all_gather(resid, 'tp', axis=0, tiled=True)  78.7 us
    all_gather x1, waiting for transfers between devices, shards(): ctx_all = lax.all_gather(ctx_local, 'ep', axis=1, tiled=True)  39.3 us
  transfers between devices with their start and end apart: 7, of which 6 were waited for; matrix products, arithmetic and copies ran while one was open for 2% of the time, Pallas kernels for 0%

profile of v1, /device:TPU:2, one launch (start us, length us, event | category | flops | bytes accessed | tf_op | source)
XLA Modules:
  0.0 1090.3 jit_solution(11343329542706530227)
XLA Ops:
  7.2 0.9 fusion.32
  8.1 150.2 %psum.28 = f32[256]{0:T(256)S(1)} all-reduce(f32[256]{0:T(256)S(1)} %fusion.32), channel_id=1, replica_groups=mesh['tp'=64,'ep'=8] {'tp'}, use_global_device_ids=true, to_apply=%region_1.0 | all-reduce | flops 256 | bytes 2048 | tf_op jit(solution)/shard_map/psum | solution.py:50
  158.3 0.7 iota_compare_fusion.1
  159.1 1.6 fusion.9
  160.7 5.7 all-to-all-start.1
  166.5 1.6 fusion.11
  168.1 3.1 all-to-all-done.1
  171.2 4.7 all-to-all-start
  175.9 1.0 fusion.16
  177.0 2.1 fusion.19
  179.1 1.7 all-to-all-done
  180.7 2.0 fusion.21
  182.8 554.5 %all-reduce.3.cloned.1.call-done = (f32[64,2048]{1,0:T(8,128)}, f32[64,2048]{1,0:T(8,128)}, f32[64,2048]{1,0:T(8,128)}) async-done(((f32[64,2048]{1,0:T(8,128)}, f32[64,2048]{1,0:T(8,128)}, f32[64,2048]{1,0:T(8,128)}), (f32[64,2048]{1,0:T(8,128)}, f32[64,2048]{1,0:T(8,128)}, f32[64,2048]{1,0:T(8,128)})) %all-reduce.3.cloned.1.call-update) | async-done | bytes 1572880 | tf_op jit(solution)/shard_map/psum | solution.py:78
  737.3 1.6 multiply_convert_fusion.1
  739.6 0.5 broadcast.39
  740.1 0.7 reduce.1
  740.9 9.5 all_to_all.67
  750.9 80.4 %all-gather.2 = f32[64,1,256]{2,1,0:T(1,128)S(1)} all-gather(f32[1,1,256]{2,1,0:T(1,128)S(1)} %bitcast.114), channel_id=2, replica_groups=mesh['tp'=64,'ep'=8] {'tp'}, dimensions={0}, use_global_device_ids=true | all-gather | bytes 66560 | tf_op jit(solution)/shard_map/all_gather | solution.py:94
  831.4 0.7 fusion.31
  832.1 0.7 all-gather.9.cloned.1.call-update
  832.8 78.7 %all-gather.7.cloned.1.call-done = bf16[7168,256]{1,0:T(8,128)(2,1)} async-done(((bf16[112,256]{1,0:T(8,128)(2,1)}), bf16[7168,256]{1,0:T(8,128)(2,1)}) %all-gather.7.cloned.1.call-update) | async-done | bytes 3670032 | tf_op jit(solution)/shard_map/all_gather | solution.py:98
  911.4 6.2 copy.32
  917.7 6.5 all-to-all-start.3
  924.2 0.6 all-gather.11.cloned.1.call-update
  924.8 1.1 fusion
  925.9 1.1 fusion.1
  926.9 1.1 fusion.2
  928.0 107.2 %all-gather.9.cloned.1.call-done = bf16[7168,256]{1,0:T(8,128)(2,1)} async-done(((bf16[896,256]{1,0:T(8,128)(2,1)}), bf16[7168,256]{1,0:T(8,128)(2,1)}) %all-gather.9.cloned.1.call-update) | async-done | bytes 3670032 | tf_op jit(solution)/shard_map/all_gather | solution.py:103
  1035.2 4.3 fusion.3
  1039.5 0.8 copy.33
  1040.3 39.3 %all-gather.11.cloned.1.call-done = bf16[1,256,2048]{2,1,0:T(8,128)(2,1)} async-done(((bf16[1,256,256]{2,1,0:T(8,128)(2,1)}), bf16[1,256,2048]{2,1,0:T(8,128)(2,1)}) %all-gather.11.cloned.1.call-update) | async-done | bytes 1048592 | tf_op jit(solution)/shard_map/all_gather | solution.py:101
  1079.6 4.3 convolution_convert_fusion.3
  (32 shorter events, 1.3 us)
Async XLA Ops:
  7.2 168.8 %copy-start = (bf16[1,112,2048]{2,1,0:T(8,128)(2,1)S(1)}, bf16[1,112,2048]{2,1,0:T(8,128)(2,1)}, u32[]{:S(2)}) copy-start(bf16[1,112,2048]{2,1,0:T(8,128)(2,1)} %param.16) | copy-start | bytes 1376260
  160.7 10.5 all-to-all-start.1
  171.2 9.5 all-to-all-start
  175.9 563.3 %copy-start.1 = (bf16[1,112,2048]{2,1,0:T(8,128)(2,1)S(1)}, bf16[1,112,2048]{2,1,0:T(8,128)(2,1)}, u32[]{:S(2)}) copy-start(bf16[1,112,2048]{2,1,0:T(8,128)(2,1)} %param.17) | copy-start | bytes 1376260
  175.9 561.4 %all-reduce.3.cloned.1.call-start = ((), (), s32[]{:S(2)}) async-start(), calls=%async_computation.7 | async-start | bytes 3145728 | tf_op jit(solution)/shard_map/psum | solution.py:78
  176.9 573.6 %copy-start.4 = (bf16[1,112,256]{2,1,0:T(8,128)(2,1)S(1)}, bf16[1,112,256]{2,1,0:T(8,128)(2,1)}, u32[]{:S(2)}) copy-start(bf16[1,112,256]{2,1,0:T(8,128)(2,1)} %param.11) | copy-start | bytes 172036
  176.9 573.6 %copy-start.6 = (s32[1,8,8]{2,1,0:T(8,128)S(1)}, s32[1,8,8]{2,1,0:T(8,128)}, u32[]{:S(2)}) copy-start(s32[1,8,8]{2,1,0:T(8,128)} %param.19) | copy-start | bytes 772
  177.0 573.6 %copy-start.7 = (f32[112]{0:T(128)S(1)}, f32[112]{0:T(128)}, u32[]{:S(2)}) copy-start(f32[112]{0:T(128)} %param.13) | copy-start | bytes 1348
  177.0 654.4 %copy-start.5 = (bf16[1,112,256]{2,1,0:T(8,128)(2,1)S(1)}, bf16[1,112,256]{2,1,0:T(8,128)(2,1)}, u32[]{:S(2)}) copy-start(bf16[1,112,256]{2,1,0:T(8,128)(2,1)} %param.12) | copy-start | bytes 172036
  182.8 728.7 %all-gather.7.cloned.1.call-start = ((), (), s32[]{:S(2)}) async-start(), calls=%async_computation.4 | async-start | bytes 3727360 | tf_op jit(solution)/shard_map/all_gather | solution.py:98
  832.0 203.1 %all-gather.9.cloned.1.call-start = ((), (), s32[]{:S(2)}) async-start(), calls=%async_computation.5 | async-start | bytes 4128768 | tf_op jit(solution)/shard_map/all_gather | solution.py:103
  917.7 9.3 copy-start.2
  917.7 9.3 copy-start.3
  917.7 161.9 %all-to-all-start.3 = ((bf16[8,896,256]{1,2,0:T(8,128)(2,1)}), bf16[8,896,256]{1,2,0:T(8,128)(2,1)}, u32[]{:S(2)}, u32[]{:S(2)}) async-start(bf16[8,896,256]{1,2,0:T(8,128)(2,1)} %copy.32), calls=%async_computation.3 | async-start | bytes 7340032 | tf_op jit(solution)/shard_map/all_to_all | solution.py:99
  924.2 155.3 %all-gather.11.cloned.1.call-start = ((), (), s32[]{:S(2)}) async-start(), calls=%async_computation.6 | async-start | bytes 1179648 | tf_op jit(solution)/shard_map/all_gather | solution.py:101
Sparse Core Ops, SparseCore 0:
  182.9 554.3 all-reduce.2
  832.2 79.2 all-gather.6
  913.7 121.4 all-gather.8
  1037.2 42.2 all-gather.10
